TPU v7x, 32 devices: a whole 2x2x4 slice. The times are simulated.
32 devices in a mesh: grp: 2 (over x), tile: 8 (over z, y), mem: 2 (over core).
Axes of the slice: x: 2, y: 2, z: 4, core: 2. Of those that a mesh axis runs over, the one named last changes fastest.
Arguments:
- increment: float32 [64, 512, 512], P('grp', 'tile'), parts along dimension 0, may hold values from -6 to 6
- perturbations: bfloat16 [24, 64, 512, 512], P('mem', 'grp', 'tile'), parts along dimension 1, may hold values from -3 to 3
- localization: bfloat16 [18, 256, 256], replicated, may hold values from -1 to 3, as said below
Outputs:
- covariance_product: float32 [64, 512, 512], P('grp', 'tile', 'mem'), parts along dimension 0
There are 2 independent parts, one for each index of `grp`. A program takes and returns all parts, laid end to end along the dimension named above; an argument that names none is the same for every part. Nothing has to cross between parts.
Inputs may be any that keep to these rules, and one draw needn't show every extreme that they name: mode-dependent localization matrices.
All inputs are finite; a program needn't handle non-finite values.
Results may differ from a plain program's by a relative error of at most 0.0052.
Values may be sent and summed in bfloat16 or wider, within the bound.
No kernel may reach another device: no remote copies, remote signals or barrier semaphores. Data moves between devices by JAX's collectives and lax.ppermute only.
A program may use at most 128 MiB of HBM per device.

v0:
```python
import math
import jax
import jax.numpy as jnp
from jax import lax
from jax.sharding import PartitionSpec as P

NX = 512
NY = 512
NZ = 32
MX = 256
MY = 256
MZ = 18


def make_table(modes, cells):
    index = jnp.arange(modes, dtype=jnp.float32)[:, None]
    points = jnp.arange(cells, dtype=jnp.float32)[None, :]
    weights = jnp.where(index == 0, math.sqrt(1.0 / cells), math.sqrt(2.0 / cells))
    return (weights * jnp.cos(math.pi * index * (2.0 * points + 1.0) / (2.0 * cells))).astype(
        jnp.bfloat16
    )


def apply_localization(fields, table_x, localization):
    spectral_weights = jnp.einsum(
        "mync,kn->mcyk", fields, table_x, preferred_element_type=jnp.float32
    ).astype(jnp.bfloat16)
    localized_field = jnp.einsum(
        "aebq,efq->aebf", spectral_weights, localization, preferred_element_type=jnp.float32
    ).astype(jnp.bfloat16)
    return jnp.einsum(
        "mcyl,ln->mync", localized_field, table_x, preferred_element_type=jnp.float32
    ).astype(jnp.bfloat16)


def shards(increment, perturbations, localization):
    members, levels, tile_rows, columns = perturbations.shape
    table_y = make_table(MY, NY)
    table_z = make_table(MZ, NZ)
    table_x = make_table(MX, NX)
    product = (perturbations.astype(jnp.float32) * increment[None]).astype(jnp.bfloat16)
    along_y = jnp.einsum(
        "mzxn,yn->mzxy", product, table_y, preferred_element_type=jnp.float32
    ).astype(jnp.bfloat16)
    along_z = jnp.einsum(
        "cz,mzxy->myxc", table_z, along_y, preferred_element_type=jnp.float32
    ).astype(jnp.bfloat16)
    outgoing = along_z.reshape(members, MY, 1, tile_rows * MZ)
    received = lax.all_to_all(outgoing, "tile", split_axis=1, concat_axis=2, tiled=True)
    member_count = received.shape[0]
    block_list = received.shape[1]
    tile_count = received.shape[2]
    prolonged = apply_localization(
        received.reshape(member_count, block_list, NX, MZ), table_x, localization
    )
    parted = prolonged.reshape(member_count, block_list, tile_count, tile_rows * MZ)
    returned = lax.all_to_all(parted, "tile", split_axis=2, concat_axis=1, tiled=True)
    back = returned.reshape(members, MY, tile_rows, MZ)
    back_z = jnp.einsum("myxc,cz->mzxy", back, table_z, preferred_element_type=jnp.float32).astype(
        jnp.bfloat16
    )
    back_y = jnp.einsum("mzxy,yn->mzxn", back_z, table_y, preferred_element_type=jnp.float32)
    summed = jnp.sum(perturbations.astype(jnp.float32) * back_y, axis=0)
    output_field = lax.psum_scatter(summed, "mem", scatter_dimension=2, tiled=True)
    return output_field


def solution(mesh):
    return jax.shard_map(
        shards,
        mesh=mesh,
        in_specs=(P("grp", "tile", None), P("mem", "grp", "tile", None), P()),
        out_specs=P("grp", "tile", "mem"),
        check_vma=False,
    )
```

profile of v0, /device:TPU:0, one launch (start us, length us, event | category | flops | bytes accessed | tf_op | source)
XLA Modules:
  0.0 950.7 jit_solution(16235727651460496448)
XLA Ops:
  6.5 0.0 copy-start
  6.5 0.0 reduce-scatter.2.cloned.1.call-start
  6.6 24.8 %fusion = bf16[12,32,64,512]{3,2,1,0:T(8,128)(2,1)} fusion(bf16[12,32,64,512]{3,2,1,0:T(8,128)(2,1)} %param.4, f32[32,64,512]{2,1,0:T(8,128)} %param.3), kind=kLoop, calls=%fused_computation.2 | loop fusion | flops 37748736 | bytes 54525952 | tf_op jit(solution)/shard_map/convert_element_type | solution.py:41
  31.4 36.9 %convert_bitcast_fusion.1 = bf16[12,256,64,18]{1,3,2,0:T(8,128)(2,1)} fusion(bf16[12,32,64,512]{3,2,1,0:T(8,128)(2,1)} %fusion, f32[512]{0:T(512)S(1)} %multiply_add_fusion, f32[256]{0:T(256)S(1)} %get-tuple-element.6, f32[256]{0:T(256)S(1)} %get-tuple-element.5, f32[32]{0:T(128)S(1)} %multiply_add_fusion.1, f32[18]{0:T(128)S(1)} %get-tuple-element.8, ...), kind=kOutput, calls=%fused_computation.10 | convolution fusion | flops 6679300096 | bytes 32248080 | tf_op jit(solution)/shard_map/cz,mzxy->myxc/dot_general | solution.py:45
  68.3 12.3 %reshape.53 = bf16[12,256,1,1152]{1,3,0,2:T(8,128)(2,1)} reshape(bf16[12,256,64,18]{1,3,2,0:T(8,128)(2,1)} %convert_bitcast_fusion.1) | data formatting | bytes 14155776 | tf_op jit(solution)/shard_map/reshape | solution.py:48
  80.7 12.5 %copy.9 = bf16[12,256,1,1152]{3,0,2,1:T(8,128)(2,1)} copy(bf16[12,256,1,1152]{1,3,0,2:T(8,128)(2,1)} %reshape.53) | data formatting | bytes 14155776 | tf_op jit(solution)/shard_map/reshape | solution.py:48
  93.2 226.1 %all_to_all.30 = bf16[12,256,1,1152]{3,0,2,1:T(8,128)(2,1)} all-to-all(bf16[12,256,1,1152]{3,0,2,1:T(8,128)(2,1)} %copy.9), channel_id=1, replica_groups=mesh['grp'=2,'tile'=8,'mem'=2] {'tile'}, dimensions={1} | all-to-all | bytes 14155776 | tf_op jit(solution)/shard_map/all_to_all | solution.py:49
  319.3 5.3 copy.10
  324.7 5.7 copy.11
  330.3 123.3 %reshape.54 = bf16[12,32,512,18]{3,2,1,0:T(8,128)(2,1)} reshape(bf16[12,32,8,1,1152]{4,2,1,0,3:T(8,128)(2,1)} %copy.11) | data formatting | bytes 14155776 | tf_op jit(solution)/shard_map/reshape | solution.py:54
  453.6 43.7 %copy.12 = bf16[12,32,512,18]{2,1,3,0:T(8,128)(2,1)} copy(bf16[12,32,512,18]{3,2,1,0:T(8,128)(2,1)} %reshape.54) | data formatting | bytes 14155776 | tf_op jit(solution)/shard_map/reshape | solution.py:54
  497.3 10.2 %fusion.29 = bf16[256,12,32,18]{0,2,3,1:T(8,128)(2,1)} fusion(bf16[12,32,512,18]{2,1,3,0:T(8,128)(2,1)} %copy.12, f32[512]{0:T(512)S(1)} %multiply_add_fusion, f32[256]{0:T(256)S(1)} %get-tuple-element.6, f32[256]{0:T(256)S(1)} %get-tuple-element.5), kind=kOutput, calls=%fused_computation.20 | convolution fusion | flops 1812463616 | bytes 10620928 | tf_op jit(solution)/shard_map/mync,kn->mcyk/dot_general | solution.py:25
  507.5 0.0 copy-done
  507.5 9.5 convert_bitcast_fusion.2
  517.0 41.2 %copy.13 = bf16[12,32,512,18]{3,2,1,0:T(8,128)(2,1)} copy(bf16[12,32,512,18]{2,1,3,0:T(8,128)(2,1)} %convert_bitcast_fusion.2) | data formatting | bytes 14155776 | tf_op jit(solution)/shard_map/convert_element_type | solution.py:33
  558.2 71.0 %reshape.55 = bf16[12,32,8,1152]{3,2,1,0:T(8,128)(2,1)} reshape(bf16[12,32,512,18]{3,2,1,0:T(8,128)(2,1)} %copy.13) | data formatting | bytes 14155776 | tf_op jit(solution)/shard_map/reshape | solution.py:56
  629.2 4.0 copy.14
  633.3 158.3 %all_to_all.31 = bf16[12,32,8,1152]{3,1,0,2:T(8,128)(2,1)} all-to-all(bf16[12,32,8,1152]{3,1,0,2:T(8,128)(2,1)S(1)} %copy.14), channel_id=1, replica_groups=mesh['grp'=2,'tile'=8,'mem'=2] {'tile'}, dimensions={2} | all-to-all | bytes 14155776 | tf_op jit(solution)/shard_map/all_to_all | solution.py:57
  791.6 25.2 %copy.15 = bf16[12,8,32,1,1152]{2,1,4,0,3:T(8,128)(2,1)} copy(bf16[12,8,32,1,1152]{4,2,0,1,3:T(8,128)(2,1)} %bitcast.56) | data formatting | bytes 14155776 | tf_op jit(solution)/shard_map/all_to_all | solution.py:57
  816.8 36.4 %reshape.56 = bf16[12,256,64,18]{1,3,2,0:T(8,128)(2,1)} reshape(bf16[12,8,32,1,1152]{2,1,4,0,3:T(8,128)(2,1)} %copy.15) | data formatting | bytes 14155776 | tf_op jit(solution)/shard_map/reshape | solution.py:58
  853.1 9.0 convert_bitcast_fusion
  862.1 0.0 copy-start.1
  862.1 70.3 %fusion.1 = f32[32,64,512]{2,1,0:T(8,128)} fusion(bf16[12,32,64,512]{3,2,1,0:T(8,128)(2,1)} %param.4, bf16[12,32,64,256]{3,1,2,0:T(8,128)(2,1)} %convert_bitcast_fusion, f32[512]{0:T(512)S(1)} %multiply_add_fusion, f32[256]{0:T(256)S(1)} %get-tuple-element.6, f32[256]{0:T(256)S(1)} %get-tuple-element.5), kind=kOutput, calls=%fused_computation.3 | convolution fusion | flops 6479675392 | bytes 41947136 | tf_op jit(solution)/shard_map/mzxy,yn->mzxn/dot_general | solution.py:62
  932.5 0.0 reduce-scatter.2.cloned.1.call-update
  932.5 10.9 %reduce-scatter.2.cloned.1.call-done = f32[32,64,256]{2,1,0:T(8,128)} async-done(((f32[32,64,512]{2,1,0:T(8,128)}), f32[32,64,256]{2,1,0:T(8,128)}) %reduce-scatter.2.cloned.1.call-update) | async-done | bytes 2097168 | tf_op jit(solution)/shard_map/reduce_scatter | solution.py:64
  943.4 0.0 copy-done.1
  (4 shorter events, 0.0 us)
Async XLA Ops:
  6.5 501.0 %copy-start = (bf16[18,256,256]{2,1,0:T(8,128)(2,1)S(1)}, bf16[18,256,256]{2,1,0:T(8,128)(2,1)}, u32[]{:S(2)}) copy-start(bf16[18,256,256]{2,1,0:T(8,128)(2,1)} %param.5) | copy-start | bytes 7077892
  6.5 936.9 %reduce-scatter.2.cloned.1.call-start = ((), (), s32[]{:S(2)}) async-start(), calls=%async_computation.3 | async-start | bytes 6291456 | tf_op jit(solution)/shard_map/reduce_scatter | solution.py:64
  862.1 81.3 %copy-start.1 = (bf16[18,256,256]{2,1,0:T(8,128)(2,1)S(1)}, bf16[18,256,256]{2,1,0:T(8,128)(2,1)}, u32[]{:S(2)}) copy-start(bf16[18,256,256]{2,1,0:T(8,128)(2,1)} %param.5) | copy-start | bytes 7077892
Sparse Core Ops, SparseCore 0:
  932.6 10.7 reduce-scatter.1
where the time goes:
time: 964 us; the launch traced here: 951 us
  blocking collectives  384 us (40%)
  local copies, waits for them, and re-layouts  381 us (40%)
  matrix products  136 us (14%)
  other arithmetic  24.9 us (3%)
  between operations  13.8 us (1%)
  waiting for transfers between devices  11 us (1%)
    all_to_all x1, blocking collectives, shards(): lax.all_to_all(outgoing, 'tile', split_axis=1, concat_axis=2, tiled=True)  226 us
    reshape x2, local copies, waits for them, and re-layouts, shards(): received.reshape(member_count, block_list, NX, MZ)  167 us
    all_to_all x1, blocking collectives, shards(): lax.all_to_all(parted, 'tile', split_axis=2, concat_axis=1, tiled=True)  158 us
    reshape x2, local copies, waits for them, and re-layouts, shards(): prolonged.reshape(member_count, block_list, tile_count, tile_rows * MZ)  75 us
    dot_general x1, matrix products, shards(): jnp.einsum('mzxy,yn->mzxn', back_z, table_y, preferred_element_type=jnp.f...  70.3 us
    convert_element_type x1, local copies, waits for them, and re-layouts, apply_localization(): return jnp.einsum('mcyl,ln->mync', localized_field, table_x, preferred_el...  41.2 us
    dot_general x1, matrix products, shards(): jnp.einsum('cz,mzxy->myxc', table_z, along_y, preferred_element_type=jnp....  36.9 us
    reshape x1, local copies, waits for them, and re-layouts, shards(): back = returned.reshape(members, MY, tile_rows, MZ)  36.4 us
  transfers between devices with their start and end apart: 1, of which 1 were waited for; matrix products, arithmetic and copies ran while one was open for 0% of the time, Pallas kernels for 0%

commit v1 on v0

--- a/solution.py
+++ b/solution.py
@@ -54,7 +54,10 @@
         received.reshape(member_count, block_list, NX, MZ), table_x, localization
     )
     parted = prolonged.reshape(member_count, block_list, tile_count, tile_rows * MZ)
-    returned = lax.all_to_all(parted, "tile", split_axis=2, concat_axis=1, tiled=True)
+    high = jnp.split(parted, lax.axis_size("tile"), axis=2)
+    heard = jnp.stack(high, 0)
+    oldest = lax.all_to_all(heard, concat_axis=0, split_axis=0, axis_name="tile")
+    returned = jnp.concatenate(oldest, 1)
     back = returned.reshape(members, MY, tile_rows, MZ)
     back_z = jnp.einsum("myxc,cz->mzxy", back, table_z, preferred_element_type=jnp.float32).astype(
         jnp.bfloat16

time: 964 us -> 982 us (1.019)
  local copies, waits for them, and re-layouts: 381 us -> 412 us
  blocking collectives: 384 us -> 372 us
    another operation x0 -> x2, local copies, waits for them, and re-layouts: none -> 36.6 us  [the longest x1 36.4 us: shards(): back = returned.reshape(members, MY, tile_rows, MZ)]
    split x0 -> x1, local copies, waits for them, and re-layouts: none -> 33.8 us  [shards(): high = jnp.split(parted, lax.axis_size('tile'), axis=2)]
    all_to_all x1 -> x0, local copies, waits for them, and re-layouts: 25.2 us -> none  [shards(): lax.all_to_all(parted, 'tile', split_axis=2, concat_axis=1, tiled=True)]
    all_to_all x1, blocking collectives: 226 us -> 213 us  [shards(): lax.all_to_all(outgoing, 'tile', split_axis=1, concat_axis=2, tiled=True)]
    reshape x1, local copies, waits for them, and re-layouts: 36.4 us -> 25.2 us  [shards(): returned = jnp.concatenate(oldest, 1)]
    reshape x2 -> x1, local copies, waits for them, and re-layouts: 75 us -> 71 us  [shards(): prolonged.reshape(member_count, block_list, tile_count, tile_rows * MZ)]
where the time goes in v1:
time: 982 us; the launch traced here: 969 us
  local copies, waits for them, and re-layouts  412 us (42%)
  blocking collectives  372 us (38%)
  matrix products  136 us (14%)
  other arithmetic  24.8 us (3%)
  between operations  13.7 us (1%)
  waiting for transfers between devices  10.9 us (1%)
    all_to_all x1, blocking collectives, shards(): lax.all_to_all(outgoing, 'tile', split_axis=1, concat_axis=2, tiled=True)  213 us
    reshape x2, local copies, waits for them, and re-layouts, shards(): received.reshape(member_count, block_list, NX, MZ)  167 us
    all_to_all x1, blocking collectives, shards(): lax.all_to_all(heard, concat_axis=0, split_axis=0, axis_name='tile')  158 us
    reshape x1, local copies, waits for them, and re-layouts, shards(): prolonged.reshape(member_count, block_list, tile_count, tile_rows * MZ)  71 us
    dot_general x1, matrix products, shards(): jnp.einsum('mzxy,yn->mzxn', back_z, table_y, preferred_element_type=jnp.f...  70.3 us
    convert_element_type x1, local copies, waits for them, and re-layouts, apply_localization(): return jnp.einsum('mcyl,ln->mync', localized_field, table_x, preferred_el...  41.6 us
    dot_general x1, matrix products, shards(): jnp.einsum('cz,mzxy->myxc', table_z, along_y, preferred_element_type=jnp....  36.9 us
    another operation x1, local copies, waits for them, and re-layouts, shards(): back = returned.reshape(members, MY, tile_rows, MZ)  36.4 us
  transfers between devices with their start and end apart: 1, of which 1 were waited for; matrix products, arithmetic and copies ran while one was open for 0% of the time, Pallas kernels for 0%

profile of v1, /device:TPU:0, one launch (start us, length us, event | category | flops | bytes accessed | tf_op | source)
XLA Modules:
  0.0 969.5 jit_solution(15393597450581960094)
XLA Ops:
  6.5 0.0 copy-start
  6.5 0.0 reduce-scatter.2.cloned.1.call-start
  6.6 24.8 %fusion = bf16[12,32,64,512]{3,2,1,0:T(8,128)(2,1)} fusion(bf16[12,32,64,512]{3,2,1,0:T(8,128)(2,1)} %param.4, f32[32,64,512]{2,1,0:T(8,128)} %param.3), kind=kLoop, calls=%fused_computation.2 | loop fusion | flops 37748736 | bytes 54525952 | tf_op jit(solution)/shard_map/convert_element_type | solution.py:41
  31.4 36.9 %convert_bitcast_fusion.1 = bf16[12,256,64,18]{1,3,2,0:T(8,128)(2,1)} fusion(bf16[12,32,64,512]{3,2,1,0:T(8,128)(2,1)} %fusion, f32[512]{0:T(512)S(1)} %multiply_add_fusion, f32[256]{0:T(256)S(1)} %get-tuple-element.14, f32[256]{0:T(256)S(1)} %get-tuple-element.13, f32[32]{0:T(128)S(1)} %multiply_add_fusion.1, f32[18]{0:T(128)S(1)} %get-tuple-element.16, ...), kind=kOutput, calls=%fused_computation.10 | convolution fusion | flops 6679300096 | bytes 32248080 | tf_op jit(solution)/shard_map/cz,mzxy->myxc/dot_general | solution.py:45
  68.3 12.3 %reshape.52 = bf16[12,256,1,1152]{1,3,0,2:T(8,128)(2,1)} reshape(bf16[12,256,64,18]{1,3,2,0:T(8,128)(2,1)} %convert_bitcast_fusion.1) | data formatting | bytes 14155776 | tf_op jit(solution)/shard_map/reshape | solution.py:48
  80.7 12.5 %copy.86 = bf16[12,256,1,1152]{3,0,2,1:T(8,128)(2,1)} copy(bf16[12,256,1,1152]{1,3,0,2:T(8,128)(2,1)} %reshape.52) | data formatting | bytes 14155776 | tf_op jit(solution)/shard_map/reshape | solution.py:48
  93.2 213.4 %all_to_all.20 = bf16[12,256,1,1152]{3,0,2,1:T(8,128)(2,1)} all-to-all(bf16[12,256,1,1152]{3,0,2,1:T(8,128)(2,1)} %copy.86), channel_id=1, replica_groups=mesh['grp'=2,'tile'=8,'mem'=2] {'tile'}, dimensions={1} | all-to-all | bytes 14155776 | tf_op jit(solution)/shard_map/all_to_all | solution.py:49
  306.6 5.3 copy.87
  311.9 5.7 copy.88
  317.6 123.3 %reshape.53 = bf16[12,32,512,18]{3,2,1,0:T(8,128)(2,1)} reshape(bf16[12,32,8,1,1152]{4,2,1,0,3:T(8,128)(2,1)} %copy.88) | data formatting | bytes 14155776 | tf_op jit(solution)/shard_map/reshape | solution.py:54
  440.8 43.7 %copy.89 = bf16[12,32,512,18]{2,1,3,0:T(8,128)(2,1)} copy(bf16[12,32,512,18]{3,2,1,0:T(8,128)(2,1)} %reshape.53) | data formatting | bytes 14155776 | tf_op jit(solution)/shard_map/reshape | solution.py:54
  484.6 10.2 %fusion.29 = bf16[256,12,32,18]{0,2,3,1:T(8,128)(2,1)} fusion(bf16[12,32,512,18]{2,1,3,0:T(8,128)(2,1)} %copy.89, f32[512]{0:T(512)S(1)} %multiply_add_fusion, f32[256]{0:T(256)S(1)} %get-tuple-element.14, f32[256]{0:T(256)S(1)} %get-tuple-element.13), kind=kOutput, calls=%fused_computation.28 | convolution fusion | flops 1812463616 | bytes 10620928 | tf_op jit(solution)/shard_map/mync,kn->mcyk/dot_general | solution.py:25
  494.7 0.0 copy-done
  494.7 9.5 convert_bitcast_fusion.2
  504.2 41.6 %copy.90 = bf16[12,32,512,18]{3,2,1,0:T(8,128)(2,1)} copy(bf16[12,32,512,18]{2,1,3,0:T(8,128)(2,1)} %convert_bitcast_fusion.2) | data formatting | bytes 14155776 | tf_op jit(solution)/shard_map/convert_element_type | solution.py:33
  545.8 71.0 %reshape.54 = bf16[12,32,8,1152]{3,2,1,0:T(8,128)(2,1)} reshape(bf16[12,32,512,18]{3,2,1,0:T(8,128)(2,1)} %copy.90) | data formatting | bytes 14155776 | tf_op jit(solution)/shard_map/reshape | solution.py:56
  616.9 33.8 %fusion.64 = (bf16[12,32,1,1152]{3,2,1,0:T(2,128)(2,1)S(1)}, bf16[12,32,1,1152]{3,2,1,0:T(2,128)(2,1)S(1)}, bf16[12,32,1,1152]{3,2,1,0:T(2,128)(2,1)S(1)}, bf16[...) fusion(bf16[12,32,8,1152]{3,2,1,0:T(8,128)(2,1)} %reshape.54), kind=kLoop, calls=%fused_computation.61 | loop fusion | bytes 14155776 | tf_op jit(solution)/shard_map/split | solution.py:57
  650.7 0.1 bitcast_dynamic-update-slice_fusion.7
  650.9 0.2 bitcast_dynamic-update-slice_fusion.6
  651.1 0.2 bitcast_dynamic-update-slice_fusion.5
  651.3 0.2 bitcast_dynamic-update-slice_fusion.4
  651.4 0.2 bitcast_dynamic-update-slice_fusion.3
  651.6 0.2 bitcast_dynamic-update-slice_fusion.2
  651.8 0.2 bitcast_dynamic-update-slice_fusion.1
  652.0 0.2 bitcast_dynamic-update-slice_fusion
  652.2 158.4 %all_to_all.21 = bf16[8,12,32,1,1152]{4,2,1,3,0:T(8,128)(2,1)} all-to-all(bf16[8,12,32,1,1152]{4,2,1,3,0:T(8,128)(2,1)S(1)} %bitcast_dynamic-update-slice_fusion), channel_id=1, replica_groups=mesh['grp'=2,'tile'=8,'mem'=2] {'tile'}, dimensions={0} | all-to-all | bytes 14155776 | tf_op jit(solution)/shard_map/all_to_all | solution.py:59
  810.6 25.2 %copy.91 = bf16[12,8,32,1,1152]{2,1,4,0,3:T(8,128)(2,1)} copy(bf16[12,8,32,1,1152]{4,2,0,3,1:T(8,128)(2,1)} %bitcast.70) | data formatting | bytes 14155776 | tf_op jit(solution)/shard_map/reshape | solution.py:60
  835.8 36.4 %reshape_reshape.3 = bf16[12,256,64,18]{1,3,2,0:T(8,128)(2,1)} reshape(bf16[12,8,32,1,1152]{2,1,4,0,3:T(8,128)(2,1)} %copy.91) | data formatting | bytes 14155776 | tf_op jit(solution)/shard_map/reshape;reshape | solution.py:61
  872.2 9.0 convert_bitcast_fusion
  881.1 0.0 copy-start.1
  881.2 70.3 %fusion.1 = f32[32,64,512]{2,1,0:T(8,128)} fusion(bf16[12,32,64,512]{3,2,1,0:T(8,128)(2,1)} %param.4, bf16[12,32,64,256]{3,1,2,0:T(8,128)(2,1)} %convert_bitcast_fusion, f32[512]{0:T(512)S(1)} %multiply_add_fusion, f32[256]{0:T(256)S(1)} %get-tuple-element.14, f32[256]{0:T(256)S(1)} %get-tuple-element.13), kind=kOutput, calls=%fused_computation.3 | convolution fusion | flops 6479675392 | bytes 41947136 | tf_op jit(solution)/shard_map/mzxy,yn->mzxn/dot_general | solution.py:65
  951.5 0.0 reduce-scatter.2.cloned.1.call-update
  951.5 10.9 %reduce-scatter.2.cloned.1.call-done = f32[32,64,256]{2,1,0:T(8,128)} async-done(((f32[32,64,512]{2,1,0:T(8,128)}), f32[32,64,256]{2,1,0:T(8,128)}) %reduce-scatter.2.cloned.1.call-update) | async-done | bytes 2097168 | tf_op jit(solution)/shard_map/reduce_scatter | solution.py:67
  962.4 0.0 copy-done.1
  (4 shorter events, 0.0 us)
Async XLA Ops:
  6.5 488.2 %copy-start = (bf16[18,256,256]{2,1,0:T(8,128)(2,1)S(1)}, bf16[18,256,256]{2,1,0:T(8,128)(2,1)}, u32[]{:S(2)}) copy-start(bf16[18,256,256]{2,1,0:T(8,128)(2,1)} %param.5) | copy-start | bytes 7077892
  6.5 955.9 %reduce-scatter.2.cloned.1.call-start = ((), (), s32[]{:S(2)}) async-start(), calls=%async_computation.3 | async-start | bytes 6291456 | tf_op jit(solution)/shard_map/reduce_scatter | solution.py:67
  881.1 81.3 %copy-start.1 = (bf16[18,256,256]{2,1,0:T(8,128)(2,1)S(1)}, bf16[18,256,256]{2,1,0:T(8,128)(2,1)}, u32[]{:S(2)}) copy-start(bf16[18,256,256]{2,1,0:T(8,128)(2,1)} %param.5) | copy-start | bytes 7077892
Sparse Core Ops, SparseCore 0:
  951.6 10.7 reduce-scatter.1
